TPU v7x, 1024 devices: a whole 8x8x8 slice. The times are simulated.
1024 devices in a mesh: row: 16 (over x, core), col: 64 (over y, z).
Axes of the slice: x: 8, y: 8, z: 8, core: 2. Of those that a mesh axis runs over, the one named last changes fastest.
Arguments:
- inputs: bfloat16 [2048, 6144], P(('row', 'col')), may hold values from -6 to 6
- cotangent: bfloat16 [2048, 6144], P(('row', 'col')), may hold values from -0.41992188 to 0.41992188
- w_in: bfloat16 [1536, 24576], P('row', 'col'), may hold values from -0.15625 to 0.15625
- w_out: bfloat16 [1536, 24576], P('row', 'col'), may hold values from -0.078125 to 0.078125
- keep_in: int32 [192, 12], replicated, may hold values from 0 to 47, all different within a row
- keep_out: int32 [192, 12], replicated, may hold values from 0 to 47, all different within a row
Outputs:
- grad_in: bfloat16 [1536, 24576], P('row', 'col')
- grad_out: bfloat16 [1536, 24576], P('row', 'col')
Inputs may be any that keep to these rules, and one draw needn't show every extreme that they name: `keep_in`: each row names 12 different input blocks, and every block is named by some row. `keep_out`: each row names 12 different output blocks, and every block is named by some row.
All inputs are finite; a program needn't handle non-finite values.
Results may differ from a plain program's by a relative error of at most 0.022.
Values may be sent and summed in bfloat16 or wider, within the bound.
A program may use at most 32 MiB of HBM per device.

v0:
```python
import jax
import jax.numpy as jnp
from jax import lax
from jax.sharding import PartitionSpec as P

D = 6144
BLK = 128
KEEP = 12


def gelu_tanh(values):
    return jax.nn.gelu(values, approximate=True)


def pick_one(matrix, chosen):
    return jnp.take(matrix, chosen, axis=1)


def per_device(inputs, cotangent, w_in, w_out, keep_in, keep_out):
    width = w_in.shape[1]
    blocks_here = width // BLK
    kept_rows = w_in.shape[0]
    column = lax.axis_index("col")
    own_in = lax.dynamic_slice_in_dim(keep_in, column * blocks_here, blocks_here, 0)
    own_out = lax.dynamic_slice_in_dim(keep_out, column * blocks_here, blocks_here, 0)
    tables = jnp.stack((own_in, own_out), 0)
    stacked = jnp.stack((inputs, cotangent), 0)
    whole = lax.all_gather(stacked, "col", axis=1, tiled=True)
    tokens_here = whole.shape[1]
    blocks = whole.reshape(2, tokens_here, D // BLK, BLK)
    picked = jax.vmap(pick_one)(blocks, tables).reshape(2, tokens_here, blocks_here, KEEP * BLK)
    weights = jnp.stack((w_in, w_out), 1)
    full = lax.all_gather(weights, "row", axis=0, tiled=True)
    panel = full.reshape(KEEP * BLK, 2, blocks_here, BLK)
    mixed = jnp.einsum("ptck,kpcq->ptcq", picked, panel, preferred_element_type=jnp.float32)
    hidden = mixed[0].reshape(tokens_here, width)
    d_act = mixed[1].reshape(tokens_here, width)
    act, pullback = jax.vjp(gelu_tanh, hidden)
    d_hidden = pullback(d_act)[0].astype(jnp.bfloat16)
    act = act.astype(jnp.bfloat16)
    paired = jnp.stack((d_hidden, act), 0).reshape(2, tokens_here, blocks_here, BLK)
    term = jnp.einsum("ptck,ptcq->kpcq", picked, paired, preferred_element_type=jnp.float32)
    summed = (
        lax.psum_scatter(
            term.reshape(lax.axis_size("row") * kept_rows, 2 * width).astype(jnp.bfloat16),
            "row",
            scatter_dimension=0,
            tiled=True,
        )
        .astype(jnp.float32)
        .reshape(kept_rows, 2, width)
    )
    return (summed[:, 0].astype(jnp.bfloat16), summed[:, 1].astype(jnp.bfloat16))


def solution(mesh):
    in_specs = (
        P(("row", "col"), None),
        P(("row", "col"), None),
        P("row", "col"),
        P("row", "col"),
        P(),
        P(),
    )
    out_specs = (P("row", "col"), P("row", "col"))
    return jax.shard_map(
        per_device, mesh=mesh, in_specs=in_specs, out_specs=out_specs, check_vma=False
    )
```

profile of v0, /device:TPU:1, one launch (start us, length us, event | category | flops | bytes accessed | tf_op | source)
XLA Modules:
  0.0 259.5 jit_solution(12239956942404977179)
XLA Ops:
  7.2 0.0 all-gather.3.cloned.1.call-start
  7.2 1.6 pad_maximum_fusion
  8.8 0.0 all-gather.3.cloned.1.call-update
  8.8 0.0 all-gather.5.cloned.1.call-start
  8.9 0.8 pad_maximum_fusion.1
  9.7 0.7 copy.38
  10.4 0.0 all-gather.5.cloned.1.call-update
  10.4 0.0 reduce-scatter.2.cloned.1.call-start
  10.4 0.8 constant_dynamic-slice_fusion
  11.3 0.1 copy.37
  11.4 0.1 copy.36
  11.5 0.1 reshape.127
  11.6 0.1 broadcast_in_dim.14
  11.7 56.5 %all-gather.3.cloned.1.call-done = bf16[1536,2,384]{2,0,1:T(8,128)(2,1)} async-done(((bf16[96,2,384]{2,0,1:T(8,128)(2,1)}), bf16[1536,2,384]{2,0,1:T(8,128)(2,1)}) %all-gather.3.cloned.1.call-update) | async-done | bytes 2359312 | tf_op jit(solution)/shard_map/all_gather | solution.py:33
  68.2 4.3 %copy.35 = bf16[1536,2,384]{0,2,1:T(8,128)(2,1)} copy(bf16[1536,2,384]{2,0,1:T(8,128)(2,1)} %all-gather.3.cloned.1.call-done) | data formatting | bytes 4718592 | tf_op jit(solution)/shard_map/all_gather | solution.py:33
  72.5 89.1 %all-gather.5.cloned.1.call-done = bf16[2,128,6144]{2,0,1:T(2,128)(2,1)} async-done(((bf16[2,2,6144]{2,0,1:T(2,128)(2,1)}), bf16[2,128,6144]{2,0,1:T(2,128)(2,1)}) %all-gather.5.cloned.1.call-update) | async-done | bytes 3145744 | tf_op jit(solution)/shard_map/all_gather | solution.py:28
  161.6 7.3 %copy.39 = bf16[2,128,6144]{1,2,0:T(8,128)(2,1)S(1)} copy(bf16[2,128,6144]{2,0,1:T(2,128)(2,1)} %all-gather.5.cloned.1.call-done) | data formatting | bytes 6291456 | tf_op jit(solution)/shard_map/all_gather | solution.py:28
  168.9 2.8 %copy.42 = bf16[2,128,48,128]{3,1,2,0:T(8,128)(2,1)} copy(bf16[2,128,48,128]{1,3,2,0:T(8,128)(2,1)S(1)} %bitcast.32) | data formatting | bytes 6291456 | tf_op jit(solution)/shard_map/reshape | solution.py:30
  171.7 3.3 %gather_fusion = bf16[72,128,128]{2,1,0:T(8,128)(2,1)S(1)} fusion(bf16[2,128,48,128]{3,1,2,0:T(8,128)(2,1)} %copy.42, s32[72]{0:T(128)S(1)} %reshape.127), kind=kCustom, calls=%fused_computation | custom fusion | bytes 4719168 | tf_op jit(solution)/shard_map/vmap(jit(_take))/gather | solution.py:16
  175.1 2.5 copy.43
  177.6 0.0 copy-start
  177.6 4.4 %bitcast_select_fusion = bf16[2,128,3,1536]{1,3,2,0:T(8,128)(2,1)S(1)} fusion(bf16[2,128,3,12,128]{1,4,3,2,0:T(8,128)(2,1)} %copy.43, pred[2,3,1536]{2,1,0:T(4,128)(4,1)S(1)} %broadcast_in_dim.15), kind=kLoop, calls=%fused_computation.2 | loop fusion | flops 1179648 | bytes 4727808 | tf_op jit(solution)/shard_map/vmap(jit(_take))/select_n | solution.py:16
  181.9 0.0 copy-done
  181.9 0.8 convolution_bitcast_fusion
  182.7 0.2 fusion.6
  182.9 0.8 convolution_convert_fusion
  183.7 2.4 copy.46
  186.1 0.0 reduce-scatter.2.cloned.1.call-update
  186.1 64.4 %reduce-scatter.2.cloned.1.call-done = bf16[96,768]{1,0:T(8,128)(2,1)} async-done(((bf16[1536,768]{1,0:T(8,128)(2,1)}), bf16[96,768]{1,0:T(8,128)(2,1)}) %reduce-scatter.2.cloned.1.call-update) | async-done | bytes 147472 | tf_op jit(solution)/shard_map/reduce_scatter | solution.py:44
  250.5 0.9 reshape.126
  251.5 0.2 fusion.14
  251.7 0.6 copy.53
  252.3 0.6 copy.54
  (3 shorter events, 0.0 us)
Async XLA Ops:
  7.2 61.0 %all-gather.3.cloned.1.call-start = ((), (), s32[]{:S(2)}) async-start(), calls=%async_computation.1 | async-start | bytes 2506752 | tf_op jit(solution)/shard_map/all_gather | solution.py:33
  8.8 152.7 %all-gather.5.cloned.1.call-start = ((), (), s32[]{:S(2)}) async-start(), calls=%async_computation.2 | async-start | bytes 3194880 | tf_op jit(solution)/shard_map/all_gather | solution.py:28
  10.4 240.1 %reduce-scatter.2.cloned.1.call-start = ((), (), s32[]{:S(2)}) async-start(), calls=%async_computation.3 | async-start | bytes 2506752 | tf_op jit(solution)/shard_map/reduce_scatter | solution.py:44
  177.6 4.4 %copy-start = (bf16[1536,2,384]{0,2,1:T(8,128)(2,1)S(1)}, bf16[1536,2,384]{0,2,1:T(8,128)(2,1)}, u32[]{:S(2)}) copy-start(bf16[1536,2,384]{0,2,1:T(8,128)(2,1)} %copy.35) | copy-start | bytes 7077892
Sparse Core Ops, SparseCore 0:
  10.7 57.4 all-gather.2
  73.0 88.5 all-gather.4
  186.2 64.2 reduce-scatter.1
where the time goes:
time: 260 us
  waiting for transfers between devices  210 us (81%)
  local copies, waits for them, and re-layouts  27 us (10%)
  between operations  13.8 us (5%)
  other arithmetic  6.96 us (3%)
    all_gather x1, waiting for transfers between devices, per_device(): whole = lax.all_gather(stacked, 'col', axis=1, tiled=True)  89.1 us
    reduce_scatter x1, waiting for transfers between devices, per_device(): lax.psum_scatter(term.reshape(lax.axis_size('row') * kept_rows, 2 * width...  64.4 us
    all_gather x1, waiting for transfers between devices, per_device(): full = lax.all_gather(weights, 'row', axis=0, tiled=True)  56.5 us
    all_gather x1, local copies, waits for them, and re-layouts, per_device(): whole = lax.all_gather(stacked, 'col', axis=1, tiled=True)  7.33 us
    gather x3, local copies, waits for them, and re-layouts, pick_one(): return jnp.take(matrix, chosen, axis=1)  5.88 us
  transfers between devices with their start and end apart: 3, of which 3 were waited for; matrix products, arithmetic and copies ran while one was open for 3% of the time, Pallas kernels for 0%

commit v1 on v0

v1 whole, which is shorter than its diff:
```python
import functools
import math

import jax
import jax.numpy as jnp
from jax import lax
from jax.experimental import pallas as pl
from jax.experimental.pallas import tpu as pltpu
from jax.sharding import PartitionSpec as P

BLK = 128
MESH = pl.DeviceIdType.MESH
RIGHT, LEFT = 0, 1
SIGN = (1, -1)
FAN = 2


def gelu_terms(hidden):
    scale = math.sqrt(2.0 / math.pi)
    square = hidden * hidden
    curve = jnp.tanh(scale * (hidden + 0.044715 * (square * hidden)))
    half = 0.5 * (1.0 + curve)
    slope = half + 0.5 * hidden * (1.0 - curve * curve) * (scale * (1.0 + 3 * 0.044715 * square))
    return hidden * half, slope


def body(
    nx,
    n,
    x_hbm,
    c_hbm,
    wi_hbm,
    wo_hbm,
    keep_in,
    keep_out,
    gi_ref,
    go_ref,
    gat,
    t32,
    tok_in,
    tok_out,
    wts,
    picked,
    grads,
    sib,
    part,
    land,
    dh,
    act,
    local_sem,
    p1_send,
    p1_recv,
    ring_send,
    ring_recv,
    pair_send,
    pair_recv,
    sib_send,
    sib_recv,
    sum_send,
    sum_recv,
):
    row, col = lax.axis_index("row"), lax.axis_index("col")
    x, core = row // 2, lax.rem(row, 2)
    y, z = col // n, lax.rem(col, n)
    kept, width = wi_hbm.shape
    nb = width // BLK
    tok = (tok_in, tok_out)
    blocks, per_tile, _ = tok_in[0].shape
    tokens = n * per_tile
    half_blocks = blocks // FAN
    keeps = (keep_in, keep_out)
    sibling = (2 * x + 1 - core, col)
    hx, hn = nx // 2, n // 2

    def wrap(at, by, size):
        return lax.rem(at + by % size, size)

    def z_peer(d):
        return (row, y * n + wrap(z, d, n))

    def y_peer(d):
        return (row, wrap(y, d, n) * n + z)

    def x_peer(d):
        return (2 * wrap(x, d, nx) + core, col)

    peers = [z_peer(d) for d in range(1, n)] + [y_peer(d) for d in range(1, n)]
    peers += [x_peer(d) for d in sorted({1, nx - 1})] + [sibling]

    barrier = pltpu.get_barrier_semaphore()
    for peer in peers:
        pl.semaphore_signal(barrier, inc=1, device_id=peer, device_id_type=MESH)
    pl.semaphore_wait(barrier, len(peers))

    sends = []

    def send(src, dst, s_sem, r_sem, device):
        copy = pltpu.make_async_remote_copy(
            src_ref=src, dst_ref=dst, send_sem=s_sem, recv_sem=r_sem, device_id=device, device_id_type=MESH
        )
        copy.start()
        sends.append(copy)

    def arrived(ref, r_sem, s_sem):
        pltpu.make_async_remote_copy(
            src_ref=ref, dst_ref=ref, send_sem=s_sem, recv_sem=r_sem, device_id=sibling, device_id_type=MESH
        ).wait_recv()

    ring_size = (n, n, nx)
    ring_peer = (y_peer, z_peer, x_peer)

    def weight_rows(dist, whose):
        start = pl.multiple_of((2 * wrap(x, dist, nx) + whose) * kept, kept)
        return pl.ds(start, kept)

    def piece(ring, dist, part_at):
        if ring == 2:
            return wts.at[part_at, weight_rows(dist, core), :]
        return tok[ring][dist % n].at[pl.ds(part_at * half_blocks, half_blocks)]

    def ring_start(ring, way, step, part_at, src=None):
        ref = piece(ring, -(step - 1) * SIGN[way], part_at)
        send(
            ref if src is None else src,
            ref if ring == 2 else piece(ring, -step * SIGN[way], part_at),
            ring_send.at[ring, way, step - 1, part_at],
            ring_recv.at[ring, way, step - 1, part_at],
            ring_peer[ring](SIGN[way]),
        )

    def ring_takes(ring, way, step, part_at):
        top = ring_size[ring] // 2
        return step < top or (step == top and part_at == way)

    def pair_start(dist_at, dist, part_at, src=None):
        ref = wts.at[part_at, weight_rows(dist, core), :]
        send(
            ref if src is None else src,
            ref,
            pair_send.at[dist_at, part_at],
            pair_recv.at[dist_at, part_at],
            sibling,
        )

    def place(array, dist):
        first = col * nb
        at = slice(dist % n * per_tile, (dist % n + 1) * per_tile)

        def one(c, carry):
            for s in range(keep_in.shape[1]):
                block = keeps[array][first + c, s]
                picked[array, c, at, s * BLK : (s + 1) * BLK] = tok[array][dist % n][block]
            return carry

        lax.fori_loop(0, nb, one, 0)

    local = [
        pltpu.make_async_copy(x_hbm, gat.at[0, 0], local_sem.at[0]),
        pltpu.make_async_copy(c_hbm, gat.at[1, 0], local_sem.at[1]),
        pltpu.make_async_copy(wi_hbm, wts.at[0, weight_rows(0, core), :], local_sem.at[2]),
        pltpu.make_async_copy(wo_hbm, wts.at[1, weight_rows(0, core), :], local_sem.at[3]),
    ]
    for copy in local:
        copy.start()
    order = sorted(range(1, n), key=lambda d: -min(d, n - d))
    for d in order:
        for array, (src, peer) in enumerate(((x_hbm, z_peer), (c_hbm, y_peer))):
            send(src, gat.at[array, n - d], p1_send.at[array, d], p1_recv.at[array, n - d], peer(d))
    for part_at, src in enumerate((wi_hbm, wo_hbm)):
        for way in (RIGHT, LEFT):
            if ring_takes(2, way, 1, part_at):
                ring_start(2, way, 1, part_at, src)
        pair_start(0, 0, part_at, src)

    for array in (0, 1):
        for d in [0] + order[::-1]:
            if d == 0:
                local[array].wait()
            else:
                arrived(gat.at[array, d], p1_recv.at[array, d], p1_send.at[array, d])
            t32[array, 2 * d : 2 * d + 2, :] = gat[array, d].astype(jnp.float32)
        for b in range(blocks):
            tok[array][0][b] = t32[array, :, b * BLK : (b + 1) * BLK].astype(jnp.bfloat16)
        for part_at in range(FAN):
            for way in (RIGHT, LEFT):
                if ring_takes(array, way, 1, part_at):
                    ring_start(array, way, 1, part_at)
    for array in (0, 1):
        place(array, 0)

    for step in range(1, max(hx, hn) + 1):
        for part_at in range(FAN):
            for ring in (2, 0, 1):
                for way in (RIGHT, LEFT):
                    if not ring_takes(ring, way, step, part_at):
                        continue
                    dist = -step * SIGN[way]
                    ref = piece(ring, dist, part_at)
                    arrived(ref, ring_recv.at[ring, way, step - 1, part_at], ring_send.at[ring, way, step - 1, part_at])
                    if ring_takes(ring, way, step + 1, part_at):
                        ring_start(ring, way, step + 1, part_at)
                    if ring == 2:
                        pair_start(step + way * hx, dist, part_at)
        for array in (0, 1):
            if step < hn:
                place(array, step)
                place(array, -step)
            elif step == hn:
                place(array, step)

    def pair_dists():
        for part_at in range(FAN):
            yield 0, 0, part_at
            for step in range(1, hx + 1):
                for way in (RIGHT, LEFT):
                    if ring_takes(2, way, step, part_at):
                        yield step + way * hx, -step * SIGN[way], part_at

    for dist_at, dist, part_at in pair_dists():
        arrived(
            wts.at[part_at, weight_rows(dist, 1 - core), :],
            pair_recv.at[dist_at, part_at],
            pair_send.at[dist_at, part_at],
        )
    local[2].wait()
    local[3].wait()

    r_at = lax.broadcasted_iota(jnp.int32, (tokens, tokens), 0)
    c_at = lax.broadcasted_iota(jnp.int32, (tokens, tokens), 1)
    r_y, r_z = r_at // per_tile, lax.rem(r_at, per_tile) // 2
    c_z, c_y = c_at // per_tile, lax.rem(c_at, per_tile) // 2
    same = (r_y == c_y) & (r_z == c_z) & (lax.rem(r_at, 2) == lax.rem(c_at, 2))
    swap = jnp.where(same, 1.0, 0.0)
    swap_half = swap.astype(jnp.bfloat16)
    across = (((0,), (0,)), ((), ()))
    for c in range(nb):
        lanes = slice(c * BLK, (c + 1) * BLK)
        hidden = jnp.dot(picked[0, c], wts[0, :, lanes], preferred_element_type=jnp.float32)
        d_act = jnp.dot(picked[1, c], wts[1, :, lanes], preferred_element_type=jnp.float32)
        d_act = jnp.dot(swap, d_act, preferred_element_type=jnp.float32, precision=lax.Precision.HIGHEST)
        value, slope = gelu_terms(hidden)
        dh[:, lanes] = (d_act * slope).astype(jnp.bfloat16)
        act[:, lanes] = lax.dot_general(
            swap_half, value.astype(jnp.bfloat16), across, preferred_element_type=jnp.float32
        ).astype(jnp.bfloat16)
    for c in range(nb):
        lanes = slice(c * BLK, (c + 1) * BLK)
        for array, right in enumerate((dh, act)):
            grads[array, :, lanes] = lax.dot_general(
                picked[array, c], right[:, lanes], across, preferred_element_type=jnp.float32
            ).astype(jnp.bfloat16)

    offsets = [hx] + [sign * d for d in range(hx - 1, 0, -1) for sign in SIGN] + [0]

    for at, dist in enumerate(offsets):
        send(
            grads.at[:, weight_rows(dist, 1 - core), :],
            sib.at[at],
            sib_send.at[at],
            sib_recv.at[at],
            sibling,
        )

    slot_of = {dist: at for at, dist in enumerate(offsets)}
    slot_of[-hx] = slot_of[hx]

    def sum_start(way, dist, array):
        src = part.at[slot_of[dist * SIGN[way]], array]
        send(
            src,
            land.at[way, dist - 1, array],
            sum_send.at[way, dist - 1, array],
            sum_recv.at[way, dist - 1, array],
            x_peer(SIGN[way]),
        )

    def first_hop(way, array):
        return hx if array == way else hx - 1

    for at, dist in enumerate(offsets):
        arrived(sib.at[at], sib_recv.at[at], sib_send.at[at])
        for array in (0, 1):
            own = grads[array, weight_rows(dist, core), :].astype(jnp.float32)
            part[at, array] = (own + sib[at, array].astype(jnp.float32)).astype(jnp.bfloat16)
        for array in (0, 1):
            for way in (RIGHT, LEFT):
                far = first_hop(way, array)
                if far >= 1 and (dist == far * SIGN[way] or (far == hx and dist == hx)):
                    sum_start(way, far, array)

    for dist in range(hx - 1, 0, -1):
        for which in (0, 1):
            for way in (RIGHT, LEFT):
                array = which ^ way
                if dist + 1 > first_hop(way, array):
                    continue
                ref = land.at[way, dist, array]
                arrived(ref, sum_recv.at[way, dist, array], sum_send.at[way, dist, array])
                at = slot_of[dist * SIGN[way]]
                total = part[at, array].astype(jnp.float32) + land[way, dist, array].astype(jnp.float32)
                part[at, array] = total.astype(jnp.bfloat16)
                sum_start(way, dist, array)

    for array, out in enumerate((gi_ref, go_ref)):
        total = part[slot_of[0], array].astype(jnp.float32)
        for way in (RIGHT, LEFT):
            if first_hop(way, array) >= 1:
                ref = land.at[way, 0, array]
                arrived(ref, sum_recv.at[way, 0, array], sum_send.at[way, 0, array])
                total = total + land[way, 0, array].astype(jnp.float32)
        out[...] = total.astype(jnp.bfloat16)

    for copy in sends:
        copy.wait_send()


def per_device(inputs, cotangent, w_in, w_out, keep_in, keep_out):
    nx = lax.axis_size("row") // 2
    n = math.isqrt(lax.axis_size("col"))
    features = inputs.shape[1]
    kept, width = w_in.shape
    rows = 2 * nx * kept
    nb = width // BLK
    per_tile = 2 * n
    tokens = n * per_tile
    half = jnp.bfloat16
    any_spec = pl.BlockSpec(memory_space=pl.ANY)
    smem_spec = pl.BlockSpec(memory_space=pltpu.SMEM)
    vmem_spec = pl.BlockSpec(memory_space=pltpu.VMEM)
    dma = pltpu.SemaphoreType.DMA
    top = max(nx, n) // 2
    return pl.pallas_call(
        functools.partial(body, nx, n),
        out_shape=(jax.ShapeDtypeStruct((kept, width), half),) * 2,
        in_specs=[any_spec] * 4 + [smem_spec] * 2,
        out_specs=(vmem_spec, vmem_spec),
        scratch_shapes=[
            pltpu.VMEM((2, n, 2, features), half),
            pltpu.VMEM((2, per_tile, features), jnp.float32),
            [pltpu.VMEM((features // BLK, per_tile, BLK), half)] * n,
            [pltpu.VMEM((features // BLK, per_tile, BLK), half)] * n,
            pltpu.VMEM((2, rows, width), half),
            pltpu.VMEM((2, nb, tokens, rows), half),
            pltpu.VMEM((2, rows, width), half),
            pltpu.VMEM((nx, 2, kept, width), half),
            pltpu.VMEM((nx, 2, kept, width), half),
            pltpu.VMEM((2, nx // 2, 2, kept, width), half),
            pltpu.VMEM((tokens, width), half),
            pltpu.VMEM((tokens, width), half),
            dma((4,)),
            dma((2, n)),
            dma((2, n)),
            dma((3, 2, top, FAN)),
            dma((3, 2, top, FAN)),
            dma((nx + 1, FAN)),
            dma((nx + 1, FAN)),
            dma((nx,)),
            dma((nx,)),
            dma((2, nx // 2, 2)),
            dma((2, nx // 2, 2)),
        ],
        compiler_params=pltpu.CompilerParams(
            collective_id=0, has_side_effects=True, vmem_limit_bytes=48 * 1024 * 1024
        ),
        name="mlp_backward",
    )(inputs, cotangent, w_in, w_out, keep_in, keep_out)


def solution(mesh):
    in_specs = (
        P(("row", "col"), None),
        P(("row", "col"), None),
        P("row", "col"),
        P("row", "col"),
        P(),
        P(),
    )
    out_specs = (P("row", "col"), P("row", "col"))
    return jax.shard_map(
        per_device, mesh=mesh, in_specs=in_specs, out_specs=out_specs, check_vma=False
    )
```

time: 260 us -> 78.2 us (0.30)
  waiting for transfers between devices: 210 us -> 0 us
  Pallas kernels: 0 us -> 74.3 us
  local copies, waits for them, and re-layouts: 27 us -> 3 us
  between operations: 13.8 us -> 0.69 us
  other arithmetic: 6.96 us -> 0 us
    all_gather x2 -> x0, waiting for transfers between devices: 146 us -> none  [the longest x1 89.1 us: per_device(): whole = lax.all_gather(stacked, 'col', axis=1, tiled=True)]
    pallas_call x0 -> x1, Pallas kernels: none -> 74.3 us  [per_device(): pl.pallas_call(functools.partial(body, nx, n), out_shape=(jax.ShapeDtypeS...]
    reduce_scatter x1 -> x0, waiting for transfers between devices: 64.4 us -> none  [per_device(): lax.psum_scatter(term.reshape(lax.axis_size('row') * kept_rows, 2 * width...]
    all_gather x2 -> x0, local copies, waits for them, and re-layouts: 11.6 us -> none  [the longest x1 7.33 us: per_device(): whole = lax.all_gather(stacked, 'col', axis=1, tiled=True)]
    gather x3 -> x0, local copies, waits for them, and re-layouts: 5.88 us -> none  [pick_one(): return jnp.take(matrix, chosen, axis=1)]
    select_n x1 -> x0, other arithmetic: 4.36 us -> none  [pick_one(): return jnp.take(matrix, chosen, axis=1)]
    reshape x2 -> x0, local copies, waits for them, and re-layouts: 3.78 us -> none  [the longest x1 2.83 us: per_device(): blocks = whole.reshape(2, tokens_here, D // BLK, BLK)]
  transfers between devices with their start and end apart: 3 -> 0, of which waited for: 3 -> 0; matrix products, arithmetic and copies ran while one was open for 3% -> 0% of each run, Pallas kernels for 0% -> 0%
where the time goes in v1:
time: 78.2 us; the launch traced here: 78 us
  Pallas kernels  74.3 us (95%)
  local copies, waits for them, and re-layouts  3 us (4%)
    pallas_call x1, Pallas kernels, per_device(): pl.pallas_call(functools.partial(body, nx, n), out_shape=(jax.ShapeDtypeS...  74.3 us
    unnamed x14, local copies, waits for them, and re-layouts  3 us

profile of v1, /device:TPU:1, one launch (start us, length us, event | category | flops | bytes accessed | tf_op | source)
XLA Modules:
  0.0 78.0 jit_solution(3968372624238673375)
XLA Ops:
  0.6 0.0 copy-start.4
  0.6 0.0 copy-start.1
  0.7 0.0 copy-start.3
  0.7 0.9 %copy.8.keep_in = s32[192,12]{1,0:T(8,128)S(1)} copy(s32[192,12]{0,1:T(8,128)} %param.10) | data formatting | bytes 18432 | tf_op args[4]
  1.5 0.0 copy-done.4
  1.5 0.0 copy-start
  1.5 0.0 copy-start.2
  1.5 0.1 copy.9.keep_out
  1.7 0.0 copy-done.1
  1.7 0.0 copy-done.3
  1.7 0.7 copy-done
  2.4 0.0 copy-done.2
  2.4 74.3 %mlp_backward.1 = (bf16[96,384]{1,0:T(8,128)(2,1)S(1)}, bf16[96,384]{1,0:T(8,128)(2,1)S(1)}) custom-call(bf16[2,6144]{1,0:T(2,128)(2,1)S(1)} %copy-done.2, bf16[2,6144]{1,0:T(2,128)(2,1)S(1)} %copy-done.3, bf16[96,384]{1,0:T(8,128)(2,1)S(1)} %copy-done, bf16[96,384]{1,0:T(8,128)(2,1)S(1)} %copy-done.1, s32[192,12]{1,0:T(8,128)S(1)} %copy.8.keep_in, ...), custom_call_target="tpu_custom_call" | custom-call | tf_op jit(solution)/shard_map/mlp_backward/pallas_call | solution.py:332
  76.7 0.6 copy.12
  77.3 0.6 copy.13
Async XLA Ops:
  0.6 0.9 %copy-start.4 = (s32[192,12]{0,1:T(8,128)S(1)}, s32[192,12]{0,1:T(8,128)}, u32[]{:S(2)}) copy-start(s32[192,12]{0,1:T(8,128)} %param.11) | copy-start | bytes 27652
  0.6 1.0 %copy-start.1 = (bf16[96,384]{1,0:T(8,128)(2,1)S(1)}, bf16[96,384]{1,0:T(8,128)(2,1)}, u32[]{:S(2)}) copy-start(bf16[96,384]{1,0:T(8,128)(2,1)} %wo_hbm.1) | copy-start | bytes 221188
  0.7 1.0 %copy-start.3 = (bf16[2,6144]{1,0:T(2,128)(2,1)S(1)}, bf16[2,6144]{1,0:T(2,128)(2,1)}, u32[]{:S(2)}) copy-start(bf16[2,6144]{1,0:T(2,128)(2,1)} %c_hbm.1) | copy-start | bytes 73732
  1.5 0.9 %copy-start = (bf16[96,384]{1,0:T(8,128)(2,1)S(1)}, bf16[96,384]{1,0:T(8,128)(2,1)}, u32[]{:S(2)}) copy-start(bf16[96,384]{1,0:T(8,128)(2,1)} %wi_hbm.1) | copy-start | bytes 221188
  1.5 0.9 %copy-start.2 = (bf16[2,6144]{1,0:T(2,128)(2,1)S(1)}, bf16[2,6144]{1,0:T(2,128)(2,1)}, u32[]{:S(2)}) copy-start(bf16[2,6144]{1,0:T(2,128)(2,1)} %x_hbm.1) | copy-start | bytes 73732

commit v2 on v1

v2 whole, which is shorter than its diff:
```python
import functools
import math

import jax
import jax.numpy as jnp
from jax import lax
from jax.experimental import pallas as pl
from jax.experimental.pallas import tpu as pltpu
from jax.sharding import PartitionSpec as P

BLK = 128
MESH = pl.DeviceIdType.MESH
RIGHT, LEFT = 0, 1
SIGN = (1, -1)
FAN = 4
HALVES = 2
ROW_PARTS = 2


def gelu_terms(hidden):
    scale = math.sqrt(2.0 / math.pi)
    square = hidden * hidden
    curve = jnp.tanh(scale * (hidden + 0.044715 * (square * hidden)))
    half = 0.5 * (1.0 + curve)
    slope = half + 0.5 * hidden * (1.0 - curve * curve) * (scale * (1.0 + 3 * 0.044715 * square))
    return hidden * half, slope


def body(
    nx,
    n,
    x_hbm,
    c_hbm,
    wi_hbm,
    wo_hbm,
    keep_in_hbm,
    keep_out_hbm,
    gi_ref,
    go_ref,
    gat,
    t32,
    tok_in,
    tok_out,
    wts,
    picked,
    grads,
    sib,
    part,
    land,
    dh,
    act,
    keep_in,
    keep_out,
    local_sem,
    p1_send,
    p1_recv,
    ring_send,
    ring_recv,
    pair_send,
    pair_recv,
    sib_send,
    sib_recv,
    sum_send,
    sum_recv,
):
    row, col = lax.axis_index("row"), lax.axis_index("col")
    x, core = row // 2, lax.rem(row, 2)
    y, z = col // n, lax.rem(col, n)
    kept, width = wi_hbm.shape
    nb = width // BLK
    tok = (tok_in, tok_out)
    blocks, per_tile, _ = tok_in[0].shape
    tokens = n * per_tile
    fan_blocks = blocks // FAN
    half_blocks = blocks // HALVES
    keeps = (keep_in, keep_out)
    sibling = (2 * x + 1 - core, col)
    hx, hn = nx // 2, n // 2

    def wrap(at, by, size):
        return lax.rem(at + by % size, size)

    def z_peer(d):
        return (row, y * n + wrap(z, d, n))

    def y_peer(d):
        return (row, wrap(y, d, n) * n + z)

    def x_peer(d):
        return (2 * wrap(x, d, nx) + core, col)

    peers = [z_peer(d) for d in range(1, n)] + [y_peer(d) for d in range(1, n)]
    peers += [x_peer(d) for d in sorted({1, nx - 1})] + [sibling]

    def weight_rows(dist, whose):
        start = pl.multiple_of((2 * wrap(x, dist, nx) + whose) * kept, kept)
        return pl.ds(start, kept)

    def half_lanes(half):
        return pl.ds(half * half_blocks * BLK, half_blocks * BLK)

    local = [
        pltpu.make_async_copy(src.at[:, half_lanes(half)], gat.at[array, half, 0], local_sem.at[array, half])
        for array, src in enumerate((x_hbm, c_hbm))
        for half in range(HALVES)
    ]
    local += [
        pltpu.make_async_copy(wi_hbm, wts.at[0, weight_rows(0, core), :], local_sem.at[2, 0]),
        pltpu.make_async_copy(wo_hbm, wts.at[1, weight_rows(0, core), :], local_sem.at[2, 1]),
        pltpu.make_async_copy(keep_in_hbm, keep_in, local_sem.at[3, 0]),
        pltpu.make_async_copy(keep_out_hbm, keep_out, local_sem.at[3, 1]),
    ]
    for copy in local:
        copy.start()

    barrier = pltpu.get_barrier_semaphore()
    for peer in peers:
        pl.semaphore_signal(barrier, inc=1, device_id=peer, device_id_type=MESH)
    pl.semaphore_wait(barrier, len(peers))

    sends = []

    def send(src, dst, s_sem, r_sem, device):
        copy = pltpu.make_async_remote_copy(
            src_ref=src, dst_ref=dst, send_sem=s_sem, recv_sem=r_sem, device_id=device, device_id_type=MESH
        )
        copy.start()
        sends.append(copy)

    def arrived(ref, r_sem, s_sem):
        pltpu.make_async_remote_copy(
            src_ref=ref, dst_ref=ref, send_sem=s_sem, recv_sem=r_sem, device_id=sibling, device_id_type=MESH
        ).wait_recv()

    ring_size = (n, n, nx)
    fans = (FAN, FAN, 2)
    ring_peer = (y_peer, z_peer, x_peer)

    def piece(ring, dist, part_at):
        if ring == 2:
            return wts.at[part_at, weight_rows(dist, core), :]
        return tok[ring][dist % n].at[pl.ds(part_at * fan_blocks, fan_blocks)]

    def ring_start(ring, way, step, part_at, src=None):
        ref = piece(ring, -(step - 1) * SIGN[way], part_at)
        send(
            ref if src is None else src,
            ref if ring == 2 else piece(ring, -step * SIGN[way], part_at),
            ring_send.at[ring, way, step - 1, part_at],
            ring_recv.at[ring, way, step - 1, part_at],
            ring_peer[ring](SIGN[way]),
        )

    def ring_takes(ring, way, step, part_at):
        top = ring_size[ring] // 2
        return step < top or (step == top and part_at * 2 // fans[ring] == way)

    def pair_start(dist_at, dist, part_at, src=None):
        ref = wts.at[part_at, weight_rows(dist, core), :]
        send(
            ref if src is None else src,
            ref,
            pair_send.at[dist_at, part_at],
            pair_recv.at[dist_at, part_at],
            sibling,
        )

    def place(array, dist):
        first = col * nb
        at = slice(dist % n * per_tile, (dist % n + 1) * per_tile)

        def one(c, carry):
            for s in range(keep_in.shape[0]):
                block = keeps[array][s, first + c]
                picked[array, c, at, s * BLK : (s + 1) * BLK] = tok[array][dist % n][block]
            return carry

        lax.fori_loop(0, nb, one, 0)

    order = sorted(range(1, n), key=lambda d: -min(d, n - d))
    for half in range(HALVES):
        for d in order:
            for array, (src, peer) in enumerate(((x_hbm, z_peer), (c_hbm, y_peer))):
                send(
                    src.at[:, half_lanes(half)],
                    gat.at[array, half, n - d],
                    p1_send.at[array, half, d],
                    p1_recv.at[array, half, n - d],
                    peer(d),
                )
    for part_at, src in enumerate((wi_hbm, wo_hbm)):
        for way in (RIGHT, LEFT):
            if ring_takes(2, way, 1, part_at):
                ring_start(2, way, 1, part_at, src)
        pair_start(0, 0, part_at, src)

    for half in range(HALVES):
        for array in (0, 1):
            for d in [0] + order[::-1]:
                if d == 0:
                    local[array * HALVES + half].wait()
                else:
                    arrived(gat.at[array, half, d], p1_recv.at[array, half, d], p1_send.at[array, half, d])
                t32[array, half, 2 * d : 2 * d + 2, :] = gat[array, half, d].astype(jnp.float32)
            for b in range(half_blocks):
                tok[array][0][half * half_blocks + b] = t32[array, half, :, b * BLK : (b + 1) * BLK].astype(jnp.bfloat16)
            for part_at in range(half * FAN // HALVES, (half + 1) * FAN // HALVES):
                for way in (RIGHT, LEFT):
                    if ring_takes(array, way, 1, part_at):
                        ring_start(array, way, 1, part_at)
    for copy in local[-2:]:
        copy.wait()
    for array in (0, 1):
        place(array, 0)

    for step in range(1, max(hx, hn) + 1):
        for part_at in range(FAN):
            for ring in (2, 0, 1):
                for way in (RIGHT, LEFT):
                    if part_at >= fans[ring] or not ring_takes(ring, way, step, part_at):
                        continue
                    dist = -step * SIGN[way]
                    ref = piece(ring, dist, part_at)
                    arrived(ref, ring_recv.at[ring, way, step - 1, part_at], ring_send.at[ring, way, step - 1, part_at])
                    if ring_takes(ring, way, step + 1, part_at):
                        ring_start(ring, way, step + 1, part_at)
                    if ring == 2:
                        pair_start(step + way * hx, dist, part_at)
        for array in (0, 1):
            if step < hn:
                place(array, step)
                place(array, -step)
            elif step == hn:
                place(array, step)

    def pair_dists():
        for part_at in (0, 1):
            yield 0, 0, part_at
            for step in range(1, hx + 1):
                for way in (RIGHT, LEFT):
                    if ring_takes(2, way, step, part_at):
                        yield step + way * hx, -step * SIGN[way], part_at

    for dist_at, dist, part_at in pair_dists():
        arrived(
            wts.at[part_at, weight_rows(dist, 1 - core), :],
            pair_recv.at[dist_at, part_at],
            pair_send.at[dist_at, part_at],
        )
    for copy in local[2 * HALVES : 2 * HALVES + 2]:
        copy.wait()

    r_at = lax.broadcasted_iota(jnp.int32, (tokens, tokens), 0)
    c_at = lax.broadcasted_iota(jnp.int32, (tokens, tokens), 1)
    r_y, r_z = r_at // per_tile, lax.rem(r_at, per_tile) // 2
    c_z, c_y = c_at // per_tile, lax.rem(c_at, per_tile) // 2
    same = (r_y == c_y) & (r_z == c_z) & (lax.rem(r_at, 2) == lax.rem(c_at, 2))
    swap = jnp.where(same, 1.0, 0.0)
    swap_half = swap.astype(jnp.bfloat16)
    across = (((0,), (0,)), ((), ()))
    for c in range(nb):
        lanes = slice(c * BLK, (c + 1) * BLK)
        hidden = jnp.dot(picked[0, c], wts[0, :, lanes], preferred_element_type=jnp.float32)
        d_act = jnp.dot(picked[1, c], wts[1, :, lanes], preferred_element_type=jnp.float32)
        d_act = jnp.dot(swap, d_act, preferred_element_type=jnp.float32, precision=lax.Precision.HIGHEST)
        value, slope = gelu_terms(hidden)
        dh[:, lanes] = (d_act * slope).astype(jnp.bfloat16)
        act[:, lanes] = lax.dot_general(
            swap_half, value.astype(jnp.bfloat16), across, preferred_element_type=jnp.float32
        ).astype(jnp.bfloat16)

    groups = nx // 2
    group_rows = 4 * kept
    odd = lax.rem(x, 2)
    shifts = sorted(range(groups), key=lambda g: (-min(g, groups - g), g))

    def chip_of(shift, member):
        return 2 * lax.rem(x // 2 + shift, groups) + member

    def shard(chip, whose):
        return pl.ds(pl.multiple_of((2 * chip + whose) * kept, kept), kept)

    def group_compute(at):
        start = pl.multiple_of(lax.rem(x // 2 + shifts[at], groups) * group_rows, group_rows)
        for c in range(nb):
            lanes = slice(c * BLK, (c + 1) * BLK)
            for array, right in enumerate((dh, act)):
                grads[array, pl.ds(start, group_rows), lanes] = lax.dot_general(
                    picked[array, c, :, pl.ds(start, group_rows)],
                    right[:, lanes],
                    across,
                    preferred_element_type=jnp.float32,
                ).astype(jnp.bfloat16)
        for member in (0, 1):
            send(
                grads.at[:, shard(chip_of(shifts[at], member), 1 - core), :],
                sib.at[at, member],
                sib_send.at[at, member],
                sib_recv.at[at, member],
                sibling,
            )

    def group_sum(at):
        for member in (0, 1):
            arrived(sib.at[at, member], sib_recv.at[at, member], sib_send.at[at, member])
            to = lax.rem(2 * shifts[at] + member - odd + nx, nx)
            own = shard(chip_of(shifts[at], member), core)
            for array in (0, 1):
                total = grads[array, own, :].astype(jnp.float32) + sib[at, member, array].astype(jnp.float32)
                part[to, array] = total.astype(jnp.bfloat16)

    chunk = kept // ROW_PARTS

    def sum_start(way, dist, array, r):
        rows = pl.ds(r * chunk, chunk)
        send(
            part.at[dist * SIGN[way] % nx, array, rows],
            land.at[way, dist - 1, array, rows],
            sum_send.at[way, dist - 1, array, r],
            sum_recv.at[way, dist - 1, array, r],
            x_peer(SIGN[way]),
        )

    def sum_arrived(way, dist, array, r):
        rows = pl.ds(r * chunk, chunk)
        ref = land.at[way, dist - 1, array, rows]
        arrived(ref, sum_recv.at[way, dist - 1, array, r], sum_send.at[way, dist - 1, array, r])
        return land[way, dist - 1, array, r * chunk : (r + 1) * chunk].astype(jnp.float32)

    def first_hop(way, array):
        return hx if array == way else hx - 1

    group_compute(0)
    if groups > 1:
        group_compute(1)
    group_sum(0)
    for r in range(ROW_PARTS):
        for way in (RIGHT, LEFT):
            sum_start(way, hx, way, r)
    if groups > 1:
        for at in range(2, groups - 1):
            group_compute(at)
        for at in range(1, groups - 1):
            group_sum(at)
        if groups == 2:
            group_sum(1)
        for r in range(ROW_PARTS):
            for way in (RIGHT, LEFT):
                sum_start(way, hx - 1, 1 - way, r)
        if groups > 2:
            group_compute(groups - 1)
            group_sum(groups - 1)

    for dist in range(hx - 1, 0, -1):
        for which in (1, 0):
            for r in range(ROW_PARTS):
                for way in (RIGHT, LEFT):
                    array = which ^ way
                    if dist + 1 > first_hop(way, array):
                        continue
                    came = sum_arrived(way, dist + 1, array, r)
                    at, rows = dist * SIGN[way] % nx, slice(r * chunk, (r + 1) * chunk)
                    part[at, array, rows] = (part[at, array, rows].astype(jnp.float32) + came).astype(jnp.bfloat16)
                    sum_start(way, dist, array, r)

    for array, out in enumerate((gi_ref, go_ref)):
        for r in range(ROW_PARTS):
            rows = slice(r * chunk, (r + 1) * chunk)
            total = part[0, array, rows].astype(jnp.float32)
            for way in (1 - array, array):
                if first_hop(way, array) >= 1:
                    total = total + sum_arrived(way, 1, array, r)
            out[rows, :] = total.astype(jnp.bfloat16)

    for copy in sends:
        copy.wait_send()


def per_device(inputs, cotangent, w_in, w_out, keep_in, keep_out):
    nx = lax.axis_size("row") // 2
    n = math.isqrt(lax.axis_size("col"))
    features = inputs.shape[1]
    kept, width = w_in.shape
    rows = 2 * nx * kept
    nb = width // BLK
    per_tile = 2 * n
    tokens = n * per_tile
    half = jnp.bfloat16
    hbm_spec = pl.BlockSpec(memory_space=pltpu.HBM)
    vmem_spec = pl.BlockSpec(memory_space=pltpu.VMEM)
    dma = pltpu.SemaphoreType.DMA
    top = max(nx, n) // 2
    return pl.pallas_call(
        functools.partial(body, nx, n),
        out_shape=(jax.ShapeDtypeStruct((kept, width), half),) * 2,
        in_specs=[hbm_spec] * 6,
        out_specs=(vmem_spec, vmem_spec),
        scratch_shapes=[
            pltpu.VMEM((2, HALVES, n, 2, features // HALVES), half),
            pltpu.VMEM((2, HALVES, per_tile, features // HALVES), jnp.float32),
            [pltpu.VMEM((features // BLK, per_tile, BLK), half)] * n,
            [pltpu.VMEM((features // BLK, per_tile, BLK), half)] * n,
            pltpu.VMEM((2, rows, width), half),
            pltpu.VMEM((2, nb, tokens, rows), half),
            pltpu.VMEM((2, rows, width), half),
            pltpu.VMEM((nx // 2, 2, 2, kept, width), half),
            pltpu.VMEM((nx, 2, kept, width), half),
            pltpu.VMEM((2, nx // 2, 2, kept, width), half),
            pltpu.VMEM((tokens, width), half),
            pltpu.VMEM((tokens, width), half),
            pltpu.SMEM(keep_in.shape[::-1], jnp.int32),
            pltpu.SMEM(keep_out.shape[::-1], jnp.int32),
            dma((4, 2)),
            dma((2, HALVES, n)),
            dma((2, HALVES, n)),
            dma((3, 2, top, FAN)),
            dma((3, 2, top, FAN)),
            dma((nx + 1, 2)),
            dma((nx + 1, 2)),
            dma((nx // 2, 2)),
            dma((nx // 2, 2)),
            dma((2, nx // 2, 2, ROW_PARTS)),
            dma((2, nx // 2, 2, ROW_PARTS)),
        ],
        compiler_params=pltpu.CompilerParams(
            collective_id=0, has_side_effects=True, vmem_limit_bytes=60 * 1024 * 1024
        ),
        name="mlp_backward",
    )(inputs, cotangent, w_in, w_out, keep_in.T, keep_out.T)


def solution(mesh):
    in_specs = (
        P(("row", "col"), None),
        P(("row", "col"), None),
        P("row", "col"),
        P("row", "col"),
        P(),
        P(),
    )
    out_specs = (P("row", "col"), P("row", "col"))
    return jax.shard_map(
        per_device, mesh=mesh, in_specs=in_specs, out_specs=out_specs, check_vma=False
    )
```

time: 78.2 us -> 70.4 us (0.900)
  Pallas kernels: 74.3 us -> 67.3 us
  local copies, waits for them, and re-layouts: 3 us -> 2.19 us
    pallas_call x1, Pallas kernels: 74.3 us -> 67.3 us  [per_device(): pl.pallas_call(functools.partial(body, nx, n), out_shape=(jax.ShapeDtypeS...]
    unnamed x14 -> x4, local copies, waits for them, and re-layouts: 3 us -> 2.19 us
where the time goes in v2:
time: 70.4 us; the launch traced here: 70.1 us
  Pallas kernels  67.3 us (96%)
  local copies, waits for them, and re-layouts  2.19 us (3%)
    pallas_call x1, Pallas kernels, per_device(): pl.pallas_call(functools.partial(body, nx, n), out_shape=(jax.ShapeDtypeS...  67.3 us
    unnamed x4, local copies, waits for them, and re-layouts  2.19 us

profile of v2, /device:TPU:1, one launch (start us, length us, event | category | flops | bytes accessed | tf_op | source)
XLA Modules:
  0.0 70.1 jit_solution(15716187263546535379)
XLA Ops:
  0.6 67.3 %mlp_backward.1 = (bf16[96,384]{1,0:T(8,128)(2,1)}, bf16[96,384]{1,0:T(8,128)(2,1)}) custom-call(bf16[2,6144]{1,0:T(2,128)(2,1)} %x_hbm.1, bf16[2,6144]{1,0:T(2,128)(2,1)} %c_hbm.1, bf16[96,384]{1,0:T(8,128)(2,1)} %wi_hbm.1, bf16[96,384]{1,0:T(8,128)(2,1)} %wo_hbm.1, s32[12,192]{1,0:T(8,128)} %bitcast.2, s32[12,192]{1,0:T(8,128)} %bitcast.3), custom_call_target="tpu_custom_call" | custom-call | tf_op jit(solution)/shard_map/mlp_backward/pallas_call | solution.py:393
  67.9 0.0 copy-start
  67.9 1.6 %copy.10 = bf16[96,384]{1,0:T(8,128)(2,1)} copy(bf16[96,384]{1,0:T(8,128)(2,1)} %get-tuple-element.4) | data formatting | bytes 147456
  69.5 0.0 copy-done
  69.5 0.6 copy.11
Async XLA Ops:
  67.9 1.6 %copy-start = (bf16[96,384]{1,0:T(8,128)(2,1)S(1)}, bf16[96,384]{1,0:T(8,128)(2,1)}, u32[]{:S(2)}) copy-start(bf16[96,384]{1,0:T(8,128)(2,1)} %get-tuple-element.5) | copy-start | bytes 221188

commit v3 on v2

--- a/solution.py
+++ b/solution.py
@@ -13,7 +13,7 @@
 RIGHT, LEFT = 0, 1
 SIGN = (1, -1)
 FAN = 4
-HALVES = 2
+TILES = 2
 ROW_PARTS = 2
 
 
@@ -35,8 +35,7 @@
     wo_hbm,
     keep_in_hbm,
     keep_out_hbm,
-    gi_ref,
-    go_ref,
+    out_ref,
     gat,
     t32,
     tok_in,
@@ -69,10 +68,9 @@
     kept, width = wi_hbm.shape
     nb = width // BLK
     tok = (tok_in, tok_out)
-    blocks, per_tile, _ = tok_in[0].shape
-    tokens = n * per_tile
-    fan_blocks = blocks // FAN
-    half_blocks = blocks // HALVES
+    _, blocks, per_tile, _ = tok_in[0].shape
+    tokens = n * TILES * per_tile
+    fan_blocks = blocks * TILES // FAN
     keeps = (keep_in, keep_out)
     sibling = (2 * x + 1 - core, col)
     hx, hn = nx // 2, n // 2
@@ -96,13 +94,9 @@
         start = pl.multiple_of((2 * wrap(x, dist, nx) + whose) * kept, kept)
         return pl.ds(start, kept)
 
-    def half_lanes(half):
-        return pl.ds(half * half_blocks * BLK, half_blocks * BLK)
-
     local = [
-        pltpu.make_async_copy(src.at[:, half_lanes(half)], gat.at[array, half, 0], local_sem.at[array, half])
+        pltpu.make_async_copy(src, gat.at[array, 0], local_sem.at[array, 0])
         for array, src in enumerate((x_hbm, c_hbm))
-        for half in range(HALVES)
     ]
     local += [
         pltpu.make_async_copy(wi_hbm, wts.at[0, weight_rows(0, core), :], local_sem.at[2, 0]),
@@ -139,7 +133,8 @@
     def piece(ring, dist, part_at):
         if ring == 2:
             return wts.at[part_at, weight_rows(dist, core), :]
-        return tok[ring][dist % n].at[pl.ds(part_at * fan_blocks, fan_blocks)]
+        tile, cut = divmod(part_at, FAN // TILES)
+        return tok[ring][dist % n].at[tile, pl.ds(cut * fan_blocks, fan_blocks)]
 
     def ring_start(ring, way, step, part_at, src=None):
         ref = piece(ring, -(step - 1) * SIGN[way], part_at)
@@ -167,44 +162,39 @@
 
     def place(array, dist):
         first = col * nb
-        at = slice(dist % n * per_tile, (dist % n + 1) * per_tile)
+        top = dist % n * TILES * per_tile
 
         def one(c, carry):
             for s in range(keep_in.shape[0]):
                 block = keeps[array][s, first + c]
-                picked[array, c, at, s * BLK : (s + 1) * BLK] = tok[array][dist % n][block]
+                for tile in range(TILES):
+                    rows = slice(top + tile * per_tile, top + (tile + 1) * per_tile)
+                    picked[array, c, rows, s * BLK : (s + 1) * BLK] = tok[array][dist % n][tile, block]
             return carry
 
         lax.fori_loop(0, nb, one, 0)
 
-    order = sorted(range(1, n), key=lambda d: -min(d, n - d))
-    for half in range(HALVES):
-        for d in order:
-            for array, (src, peer) in enumerate(((x_hbm, z_peer), (c_hbm, y_peer))):
-                send(
-                    src.at[:, half_lanes(half)],
-                    gat.at[array, half, n - d],
-                    p1_send.at[array, half, d],
-                    p1_recv.at[array, half, n - d],
-                    peer(d),
-                )
+    near = sorted(range(n), key=lambda d: (min(d, n - d), d))
+    for d in near[1:]:
+        for array, (src, peer) in enumerate(((x_hbm, z_peer), (c_hbm, y_peer))):
+            send(src, gat.at[array, d], p1_send.at[array, d], p1_recv.at[array, d], peer(n - d))
     for part_at, src in enumerate((wi_hbm, wo_hbm)):
         for way in (RIGHT, LEFT):
             if ring_takes(2, way, 1, part_at):
                 ring_start(2, way, 1, part_at, src)
         pair_start(0, 0, part_at, src)
 
-    for half in range(HALVES):
+    for tile in range(TILES):
         for array in (0, 1):
-            for d in [0] + order[::-1]:
+            for at, d in enumerate(near[tile * n // TILES : (tile + 1) * n // TILES]):
                 if d == 0:
-                    local[array * HALVES + half].wait()
+                    local[array].wait()
                 else:
-                    arrived(gat.at[array, half, d], p1_recv.at[array, half, d], p1_send.at[array, half, d])
-                t32[array, half, 2 * d : 2 * d + 2, :] = gat[array, half, d].astype(jnp.float32)
-            for b in range(half_blocks):
-                tok[array][0][half * half_blocks + b] = t32[array, half, :, b * BLK : (b + 1) * BLK].astype(jnp.bfloat16)
-            for part_at in range(half * FAN // HALVES, (half + 1) * FAN // HALVES):
+                    arrived(gat.at[array, d], p1_recv.at[array, d], p1_send.at[array, d])
+                t32[array, tile, 2 * at : 2 * at + 2, :] = gat[array, d].astype(jnp.float32)
+            for b in range(blocks):
+                tok[array][0][tile, b] = t32[array, tile, :, b * BLK : (b + 1) * BLK].astype(jnp.bfloat16)
+            for part_at in range(tile * FAN // TILES, (tile + 1) * FAN // TILES):
                 for way in (RIGHT, LEFT):
                     if ring_takes(array, way, 1, part_at):
                         ring_start(array, way, 1, part_at)
@@ -247,14 +237,17 @@
             pair_recv.at[dist_at, part_at],
             pair_send.at[dist_at, part_at],
         )
-    for copy in local[2 * HALVES : 2 * HALVES + 2]:
+    for copy in local[2:4]:
         copy.wait()
 
-    r_at = lax.broadcasted_iota(jnp.int32, (tokens, tokens), 0)
-    c_at = lax.broadcasted_iota(jnp.int32, (tokens, tokens), 1)
-    r_y, r_z = r_at // per_tile, lax.rem(r_at, per_tile) // 2
-    c_z, c_y = c_at // per_tile, lax.rem(c_at, per_tile) // 2
-    same = (r_y == c_y) & (r_z == c_z) & (lax.rem(r_at, 2) == lax.rem(c_at, 2))
+    def split(at):
+        place_at = lax.rem(at, 2 * n) // 2
+        offset = jnp.where(lax.rem(place_at, 2) == 1, (place_at + 1) // 2, lax.rem(n - place_at // 2, n))
+        return at // (2 * n), offset, lax.rem(at, 2)
+
+    r_y, r_z, r_pair = split(lax.broadcasted_iota(jnp.int32, (tokens, tokens), 0))
+    c_z, c_y, c_pair = split(lax.broadcasted_iota(jnp.int32, (tokens, tokens), 1))
+    same = (r_y == c_y) & (r_z == c_z) & (r_pair == c_pair)
     swap = jnp.where(same, 1.0, 0.0)
     swap_half = swap.astype(jnp.bfloat16)
     across = (((0,), (0,)), ((), ()))
@@ -363,14 +356,14 @@
                     part[at, array, rows] = (part[at, array, rows].astype(jnp.float32) + came).astype(jnp.bfloat16)
                     sum_start(way, dist, array, r)
 
-    for array, out in enumerate((gi_ref, go_ref)):
+    for array in (0, 1):
         for r in range(ROW_PARTS):
             rows = slice(r * chunk, (r + 1) * chunk)
             total = part[0, array, rows].astype(jnp.float32)
             for way in (1 - array, array):
                 if first_hop(way, array) >= 1:
                     total = total + sum_arrived(way, 1, array, r)
-            out[rows, :] = total.astype(jnp.bfloat16)
+            out_ref[array, rows, :] = total.astype(jnp.bfloat16)
 
     for copy in sends:
         copy.wait_send()
@@ -383,23 +376,23 @@
     kept, width = w_in.shape
     rows = 2 * nx * kept
     nb = width // BLK
-    per_tile = 2 * n
-    tokens = n * per_tile
+    per_tile = 2 * n // TILES
+    tokens = 2 * n * n
     half = jnp.bfloat16
     hbm_spec = pl.BlockSpec(memory_space=pltpu.HBM)
     vmem_spec = pl.BlockSpec(memory_space=pltpu.VMEM)
     dma = pltpu.SemaphoreType.DMA
     top = max(nx, n) // 2
-    return pl.pallas_call(
+    total = pl.pallas_call(
         functools.partial(body, nx, n),
-        out_shape=(jax.ShapeDtypeStruct((kept, width), half),) * 2,
+        out_shape=jax.ShapeDtypeStruct((2, kept, width), half),
         in_specs=[hbm_spec] * 6,
-        out_specs=(vmem_spec, vmem_spec),
+        out_specs=vmem_spec,
         scratch_shapes=[
-            pltpu.VMEM((2, HALVES, n, 2, features // HALVES), half),
-            pltpu.VMEM((2, HALVES, per_tile, features // HALVES), jnp.float32),
-            [pltpu.VMEM((features // BLK, per_tile, BLK), half)] * n,
-            [pltpu.VMEM((features // BLK, per_tile, BLK), half)] * n,
+            pltpu.VMEM((2, n, 2, features), half),
+            pltpu.VMEM((2, TILES, per_tile, features), jnp.float32),
+            [pltpu.VMEM((TILES, features // BLK, per_tile, BLK), half)] * n,
+            [pltpu.VMEM((TILES, features // BLK, per_tile, BLK), half)] * n,
             pltpu.VMEM((2, rows, width), half),
             pltpu.VMEM((2, nb, tokens, rows), half),
             pltpu.VMEM((2, rows, width), half),
@@ -411,8 +404,8 @@
             pltpu.SMEM(keep_in.shape[::-1], jnp.int32),
             pltpu.SMEM(keep_out.shape[::-1], jnp.int32),
             dma((4, 2)),
-            dma((2, HALVES, n)),
-            dma((2, HALVES, n)),
+            dma((2, n)),
+            dma((2, n)),
             dma((3, 2, top, FAN)),
             dma((3, 2, top, FAN)),
             dma((nx + 1, 2)),
@@ -423,10 +416,11 @@
             dma((2, nx // 2, 2, ROW_PARTS)),
         ],
         compiler_params=pltpu.CompilerParams(
-            collective_id=0, has_side_effects=True, vmem_limit_bytes=60 * 1024 * 1024
+            collective_id=0, has_side_effects=True, vmem_limit_bytes=48 * 1024 * 1024
         ),
         name="mlp_backward",
-    )(inputs, cotangent, w_in, w_out, keep_in.T, keep_out.T)
+    )(*[pltpu.with_memory_space_constraint(v, pltpu.HBM) for v in (inputs, cotangent, w_in, w_out, keep_in.T, keep_out.T)])
+    return total[0], total[1]
 
 
 def solution(mesh):

time: 70.4 us -> 68.4 us (0.972)
  local copies, waits for them, and re-layouts: 2.19 us -> 0.67 us
    unnamed x4 -> x0, local copies, waits for them, and re-layouts: 2.19 us -> none
where the time goes in v3:
time: 68.4 us; the launch traced here: 68.2 us
  Pallas kernels  66.9 us (98%)
    pallas_call x1, Pallas kernels, per_device(): pl.pallas_call(functools.partial(body, nx, n), out_shape=jax.ShapeDtypeSt...  66.9 us

profile of v3, /device:TPU:1, one launch (start us, length us, event | category | flops | bytes accessed | tf_op | source)
XLA Modules:
  0.0 68.2 jit_solution(15427733688686788147)
XLA Ops:
  0.6 66.9 %mlp_backward.1 = bf16[2,96,384]{2,1,0:T(8,128)(2,1)S(1)} custom-call(bf16[2,6144]{1,0:T(2,128)(2,1)} %x_hbm.1, bf16[2,6144]{1,0:T(2,128)(2,1)} %c_hbm.1, bf16[96,384]{1,0:T(8,128)(2,1)} %wi_hbm.1, bf16[96,384]{1,0:T(8,128)(2,1)} %wo_hbm.1, s32[12,192]{1,0:T(8,128)} %bitcast.6, s32[12,192]{1,0:T(8,128)} %bitcast.7), custom_call_target="tpu_custom_call" | custom-call | tf_op jit(solution)/shard_map/mlp_backward/pallas_call | solution.py:386
  67.5 0.7 slice_bitcast_fusion

commit v4 on v3

--- a/solution.py
+++ b/solution.py
@@ -48,6 +48,7 @@
     land,
     dh,
     act,
+    swap,
     keep_in,
     keep_out,
     local_sem,
@@ -104,12 +105,11 @@
         pltpu.make_async_copy(keep_in_hbm, keep_in, local_sem.at[3, 0]),
         pltpu.make_async_copy(keep_out_hbm, keep_out, local_sem.at[3, 1]),
     ]
-    for copy in local:
-        copy.start()
-
     barrier = pltpu.get_barrier_semaphore()
     for peer in peers:
         pl.semaphore_signal(barrier, inc=1, device_id=peer, device_id_type=MESH)
+    for copy in local:
+        copy.start()
     pl.semaphore_wait(barrier, len(peers))
 
     sends = []
@@ -120,6 +120,10 @@
         )
         copy.start()
         sends.append(copy)
+
+    def drain(keep):
+        while len(sends) > keep:
+            sends.pop(0).wait_send()
 
     def arrived(ref, r_sem, s_sem):
         pltpu.make_async_remote_copy(
@@ -202,6 +206,16 @@
         copy.wait()
     for array in (0, 1):
         place(array, 0)
+
+    def split(at):
+        place_at = lax.rem(at, 2 * n) // 2
+        offset = jnp.where(lax.rem(place_at, 2) == 1, (place_at + 1) // 2, lax.rem(n - place_at // 2, n))
+        return at // (2 * n), offset, lax.rem(at, 2)
+
+    r_y, r_z, r_pair = split(lax.broadcasted_iota(jnp.int32, (tokens, tokens), 0))
+    c_z, c_y, c_pair = split(lax.broadcasted_iota(jnp.int32, (tokens, tokens), 1))
+    same = (r_y == c_y) & (r_z == c_z) & (r_pair == c_pair)
+    swap[...] = jnp.where(same, 1.0, 0.0).astype(jnp.bfloat16)
 
     for step in range(1, max(hx, hn) + 1):
         for part_at in range(FAN):
@@ -240,26 +254,21 @@
     for copy in local[2:4]:
         copy.wait()
 
-    def split(at):
-        place_at = lax.rem(at, 2 * n) // 2
-        offset = jnp.where(lax.rem(place_at, 2) == 1, (place_at + 1) // 2, lax.rem(n - place_at // 2, n))
-        return at // (2 * n), offset, lax.rem(at, 2)
-
-    r_y, r_z, r_pair = split(lax.broadcasted_iota(jnp.int32, (tokens, tokens), 0))
-    c_z, c_y, c_pair = split(lax.broadcasted_iota(jnp.int32, (tokens, tokens), 1))
-    same = (r_y == c_y) & (r_z == c_z) & (r_pair == c_pair)
-    swap = jnp.where(same, 1.0, 0.0)
-    swap_half = swap.astype(jnp.bfloat16)
     across = (((0,), (0,)), ((), ()))
     for c in range(nb):
         lanes = slice(c * BLK, (c + 1) * BLK)
         hidden = jnp.dot(picked[0, c], wts[0, :, lanes], preferred_element_type=jnp.float32)
         d_act = jnp.dot(picked[1, c], wts[1, :, lanes], preferred_element_type=jnp.float32)
-        d_act = jnp.dot(swap, d_act, preferred_element_type=jnp.float32, precision=lax.Precision.HIGHEST)
+        moved = jnp.zeros_like(d_act)
+        for _ in range(3):
+            head = d_act.astype(jnp.bfloat16)
+            moved = moved + jnp.dot(swap[...], head, preferred_element_type=jnp.float32)
+            d_act = d_act - head.astype(jnp.float32)
+        d_act = moved
         value, slope = gelu_terms(hidden)
         dh[:, lanes] = (d_act * slope).astype(jnp.bfloat16)
         act[:, lanes] = lax.dot_general(
-            swap_half, value.astype(jnp.bfloat16), across, preferred_element_type=jnp.float32
+            swap[...], value.astype(jnp.bfloat16), across, preferred_element_type=jnp.float32
         ).astype(jnp.bfloat16)
 
     groups = nx // 2
@@ -344,8 +353,10 @@
             group_compute(groups - 1)
             group_sum(groups - 1)
 
+    drain(4 * ROW_PARTS)
     for dist in range(hx - 1, 0, -1):
         for which in (1, 0):
+            drain(4 * ROW_PARTS)
             for r in range(ROW_PARTS):
                 for way in (RIGHT, LEFT):
                     array = which ^ way
@@ -365,8 +376,7 @@
                     total = total + sum_arrived(way, 1, array, r)
             out_ref[array, rows, :] = total.astype(jnp.bfloat16)
 
-    for copy in sends:
-        copy.wait_send()
+    drain(0)
 
 
 def per_device(inputs, cotangent, w_in, w_out, keep_in, keep_out):
@@ -401,6 +411,7 @@
             pltpu.VMEM((2, nx // 2, 2, kept, width), half),
             pltpu.VMEM((tokens, width), half),
             pltpu.VMEM((tokens, width), half),
+            pltpu.VMEM((tokens, tokens), half),
             pltpu.SMEM(keep_in.shape[::-1], jnp.int32),
             pltpu.SMEM(keep_out.shape[::-1], jnp.int32),
             dma((4, 2)),

time: 68.4 us -> 68.1 us (level)
  no operation moved by 1% of the time
where the time goes in v4:
time: 68.1 us; the launch traced here: 67.7 us
  Pallas kernels  66.4 us (98%)
    pallas_call x1, Pallas kernels, per_device(): pl.pallas_call(functools.partial(body, nx, n), out_shape=jax.ShapeDtypeSt...  66.4 us

profile of v4, /device:TPU:1, one launch (start us, length us, event | category | flops | bytes accessed | tf_op | source)
XLA Modules:
  0.0 67.7 jit_solution(9176617536174932043)
XLA Ops:
  0.6 66.4 %mlp_backward.1 = bf16[2,96,384]{2,1,0:T(8,128)(2,1)S(1)} custom-call(bf16[2,6144]{1,0:T(2,128)(2,1)} %x_hbm.1, bf16[2,6144]{1,0:T(2,128)(2,1)} %c_hbm.1, bf16[96,384]{1,0:T(8,128)(2,1)} %wi_hbm.1, bf16[96,384]{1,0:T(8,128)(2,1)} %wo_hbm.1, s32[12,192]{1,0:T(8,128)} %bitcast.6, s32[12,192]{1,0:T(8,128)} %bitcast.7), custom_call_target="tpu_custom_call" | custom-call | tf_op jit(solution)/shard_map/mlp_backward/pallas_call | solution.py:396
  67.1 0.7 slice_bitcast_fusion
